TPU v7x, 32 devices: a whole 2x2x4 slice. The times are simulated.
32 devices in a mesh: dp: 4 (over y, core), seq: 8 (over z, x).
Axes of the slice: x: 2, y: 2, z: 4, core: 2. Of those that a mesh axis runs over, the one named last changes fastest.
Arguments:
- tokens: bfloat16 [8, 1024, 2048], P('dp', 'seq'), may hold values from -6 to 6
- lengths: int32 [8], P('dp'), may hold values from 256 to 1024, as said below
- norm_gain: float32 [2048], replicated, may hold values from 0.5 to 1.5
- in_weight: bfloat16 [2048, 6144], P('seq'), may hold values from -0.125 to 0.125
- conv_taps: float32 [3, 6144], replicated, may hold values from -3 to 3
- filter_residue: float32 [2048, 16], replicated, may hold values from -0.0625 to 0.0625
- filter_decay: float32 [2048, 16], replicated, may hold values from 0.00048828125 to 0.03125
- out_weight: bfloat16 [2048, 2048], P('seq'), may hold values from -0.125 to 0.125
- feed_gain: float32 [2048], replicated, may hold values from 0.5 to 1.5
- gate_weight: bfloat16 [2048, 5632], P('seq'), may hold values from -0.125 to 0.125
- up_weight: bfloat16 [2048, 5632], P('seq'), may hold values from -0.125 to 0.125
- down_weight: bfloat16 [5632, 2048], P('seq'), may hold values from -0.078125 to 0.078125
- cotangent: bfloat16 [8, 1024, 2048], P('dp', 'seq'), may hold values from -6 to 6
Outputs:
- output: bfloat16 [8, 1024, 2048], P('dp', 'seq')
- grad_tokens: bfloat16 [8, 1024, 2048], P('dp', 'seq')
- grad_norm_gain: float32 [2048], replicated
- grad_in_weight: float32 [2048, 6144], P('seq')
- grad_conv_taps: float32 [3, 6144], replicated
- grad_filter_residue: float32 [2048, 16], replicated
- grad_filter_decay: float32 [2048, 16], replicated
- grad_out_weight: float32 [2048, 2048], P('seq')
- grad_feed_gain: float32 [2048], replicated
- grad_gate_weight: float32 [2048, 5632], P('seq')
- grad_up_weight: float32 [2048, 5632], P('seq')
- grad_down_weight: float32 [5632, 2048], P('seq')
Inputs may be any that keep to these rules, and one draw needn't show every extreme that they name: `lengths`: in each aligned block of 2 sequences (those of one index of dp) one sequence is valid to the full 1024 positions.
All inputs are finite; a program needn't handle non-finite values.
Results may differ from a plain program's by a relative error of at most 0.019.
Values may be sent and summed in bfloat16 or wider, within the bound.
No kernel may reach another device: no remote copies, remote signals or barrier semaphores. Data moves between devices by JAX's collectives and lax.ppermute only.
A program may use at most 640 MiB of HBM per device.

v0:
```python
import math
import jax
import jax.numpy as jnp
from jax import lax
from jax.sharding import PartitionSpec as P

epsilon = 1e-06
highest = lax.Precision.HIGHEST


def from_behind(shard, axis, by):
    length = lax.axis_size(axis)
    pairs = [(i, i + by) for i in range(length) if 0 <= i + by < length]
    return lax.ppermute(shard, axis, pairs)


def rms_scale(values):
    return lax.rsqrt(jnp.mean(values * values, axis=-1, keepdims=True) + epsilon)


def norm_back(values, scale, gain, grad_normed):
    grad_gain = jnp.sum(grad_normed * values * scale, axis=(0, 1))
    scaled = grad_normed * gain
    grad_values = scale * scaled - values * scale * scale * scale * jnp.mean(
        scaled * values, axis=-1, keepdims=True
    )
    return (grad_values, grad_gain)


def mode_response(residue, decay, length):
    steps = jnp.arange(length).astype(jnp.float32)
    terms = residue.T[:, None, :] * jnp.exp(-decay.T[:, None, :] * steps[None, :, None])
    return jnp.sum(terms, axis=0)


def split_size(total):
    first = 1
    for option in range(1, math.isqrt(total) + 1):
        if total % option == 0:
            first = option
    return (first, total // first)


def turn_table(rows, cols, modulus):
    index = jnp.arange(rows)[:, None] * jnp.arange(cols)[None, :] % modulus
    angle = index.astype(jnp.float32) * (2.0 * math.pi / modulus)
    return (jnp.cos(angle), jnp.sin(angle))


def complex_mix(spec, table, pair):
    real_table, imag_table = table
    real_part, imag_part = pair
    first = jnp.einsum(spec, real_table, real_part, precision=highest) - jnp.einsum(
        spec, imag_table, imag_part, precision=highest
    )
    second = jnp.einsum(spec, real_table, imag_part, precision=highest) + jnp.einsum(
        spec, imag_table, real_part, precision=highest
    )
    return (first, second)


def complex_times(one, two):
    return (one[0] * two[0] - one[1] * two[1], one[0] * two[1] + one[1] * two[0])


def conjugate(pair):
    return (pair[0], -pair[1])


def spectrum(signal, total):
    batch, length, width = signal.shape
    padded = jnp.pad(signal, ((0, 0), (0, total - length), (0, 0)))
    first, second = split_size(total)
    grid = padded.reshape(batch, second, first, width)
    cosine_inner, sine_inner = turn_table(second, second, second)
    section = (
        jnp.einsum("kn,bnmc->bkmc", cosine_inner, grid, precision=highest),
        -jnp.einsum("kn,bnmc->bkmc", sine_inner, grid, precision=highest),
    )
    cosine_twist, sine_twist = turn_table(second, first, total)
    section = complex_times(
        section, (cosine_twist[None, :, :, None], -sine_twist[None, :, :, None])
    )
    cosine_outer, sine_outer = turn_table(first, first, first)
    result = complex_mix("jm,bkmc->bjkc", (cosine_outer, -sine_outer), section)
    return (result[0].reshape(batch, total, width), result[1].reshape(batch, total, width))


def inverse(pair, total, keep):
    batch = pair[0].shape[0]
    width = pair[0].shape[2]
    first, second = split_size(total)
    grid = (
        pair[0].reshape(batch, first, second, width),
        pair[1].reshape(batch, first, second, width),
    )
    cosine_outer, sine_outer = turn_table(first, first, first)
    section = complex_mix("mj,bjkc->bmkc", (cosine_outer, sine_outer), grid)
    cosine_twist, sine_twist = turn_table(first, second, total)
    section = complex_times(section, (cosine_twist[None, :, :, None], sine_twist[None, :, :, None]))
    cosine_inner, sine_inner = turn_table(second, second, second)
    real = jnp.einsum("nk,bmkc->bnmc", cosine_inner, section[0], precision=highest) - jnp.einsum(
        "nk,bmkc->bnmc", sine_inner, section[1], precision=highest
    )
    return real.reshape(batch, total, width)[:, :keep] / total


def body(
    tokens,
    lengths,
    norm_gain,
    in_weight,
    conv_taps,
    filter_residue,
    filter_decay,
    out_weight,
    feed_gain,
    gate_weight,
    up_weight,
    down_weight,
    cotangent,
):
    parts = lax.axis_size("seq")
    local_len = tokens.shape[1]
    width = tokens.shape[2]
    full_len = local_len * parts
    channels = width // parts
    size = 2 * full_len
    place = lax.axis_index("seq")
    position = place * local_len + jnp.arange(local_len)
    mask = (position[None, :] < lengths[:, None]).astype(jnp.float32)[..., None]
    w_in, w_out, w_gate, w_up, w_down = (
        lax.all_gather(in_weight, "seq", axis=0, tiled=True),
        lax.all_gather(out_weight, "seq", axis=0, tiled=True),
        lax.all_gather(gate_weight, "seq", axis=0, tiled=True),
        lax.all_gather(up_weight, "seq", axis=0, tiled=True),
        lax.all_gather(down_weight, "seq", axis=0, tiled=True),
    )
    hidden = tokens.astype(jnp.float32)
    scale_one = rms_scale(hidden)
    normed = (hidden * scale_one * norm_gain).astype(jnp.bfloat16)
    mixed = jnp.dot(normed, w_in, preferred_element_type=jnp.float32).astype(jnp.bfloat16)
    carried = from_behind(mixed[:, local_len - 2 :, :], "seq", 1)
    extended = jnp.concatenate([carried, mixed], axis=1).astype(jnp.float32)
    short = (
        conv_taps[0] * extended[:, 2:]
        + conv_taps[1] * extended[:, 1:-1]
        + conv_taps[2] * extended[:, :-2]
    )
    query = short[..., :width]
    keys = short[..., width : 2 * width]
    values = short[..., 2 * width :]
    product = (keys * values).astype(jnp.bfloat16)
    product_chan = lax.all_to_all(product, "seq", split_axis=2, concat_axis=1, tiled=True)
    start = place * channels
    residue_part = lax.dynamic_slice_in_dim(filter_residue, start, channels, 0)
    decay_part = lax.dynamic_slice_in_dim(filter_decay, start, channels, 0)
    response = mode_response(residue_part, decay_part, full_len)
    product_spec = spectrum(product_chan.astype(jnp.float32), size)
    response_spec = spectrum(response[None], size)
    conv_chan = inverse(complex_times(product_spec, response_spec), size, full_len)
    convolved = lax.all_to_all(
        conv_chan.astype(jnp.bfloat16), "seq", split_axis=1, concat_axis=2, tiled=True
    ).astype(jnp.float32)
    gated = (query * convolved).astype(jnp.bfloat16)
    middle = hidden + jnp.dot(gated, w_out, preferred_element_type=jnp.float32)
    scale_two = rms_scale(middle)
    normed_two = (middle * scale_two * feed_gain).astype(jnp.bfloat16)
    gate = jnp.dot(normed_two, w_gate, preferred_element_type=jnp.float32)
    upper = jnp.dot(normed_two, w_up, preferred_element_type=jnp.float32)
    sigma = jax.nn.sigmoid(gate)
    active = (gate * sigma * upper).astype(jnp.bfloat16)
    feed = jnp.dot(active, w_down, preferred_element_type=jnp.float32)
    output = (mask * (middle + feed)).astype(jnp.bfloat16)
    grad_out = cotangent.astype(jnp.float32) * mask
    grad_feed = grad_out.astype(jnp.bfloat16)
    grad_active = jnp.einsum("btd,fd->btf", grad_feed, w_down, preferred_element_type=jnp.float32)
    grad_gate = (grad_active * upper * sigma * (1.0 + gate * (1.0 - sigma))).astype(jnp.bfloat16)
    grad_upper = (grad_active * gate * sigma).astype(jnp.bfloat16)
    grad_normed_two = jnp.einsum(
        "btf,df->btd", grad_gate, w_gate, preferred_element_type=jnp.float32
    ) + jnp.einsum("btf,df->btd", grad_upper, w_up, preferred_element_type=jnp.float32)
    term_gate = jnp.einsum("btd,btf->df", normed_two, grad_gate, preferred_element_type=jnp.float32)
    term_up = jnp.einsum("btd,btf->df", normed_two, grad_upper, preferred_element_type=jnp.float32)
    term_down = jnp.einsum("btf,btd->fd", active, grad_feed, preferred_element_type=jnp.float32)
    feed_terms = (
        lax.psum_scatter(
            term_gate.astype(jnp.bfloat16), "seq", scatter_dimension=0, tiled=True
        ).astype(jnp.float32),
        lax.psum_scatter(
            term_up.astype(jnp.bfloat16), "seq", scatter_dimension=0, tiled=True
        ).astype(jnp.float32),
        lax.psum_scatter(
            term_down.astype(jnp.bfloat16), "seq", scatter_dimension=0, tiled=True
        ).astype(jnp.float32),
    )
    grad_middle, grad_feed_gain = norm_back(middle, scale_two, feed_gain, grad_normed_two)
    grad_middle = grad_middle + grad_out
    grad_mix = grad_middle.astype(jnp.bfloat16)
    term_out = jnp.einsum("btd,bte->de", gated, grad_mix, preferred_element_type=jnp.float32)
    grad_gated = jnp.einsum("bte,de->btd", grad_mix, w_out, preferred_element_type=jnp.float32)
    grad_query = grad_gated * convolved
    grad_conv = (grad_gated * query).astype(jnp.bfloat16)
    grad_conv_chan = lax.all_to_all(
        grad_conv, "seq", split_axis=2, concat_axis=1, tiled=True
    ).astype(jnp.float32)
    grad_spec = spectrum(grad_conv_chan, size)
    grad_product_chan = inverse(complex_times(grad_spec, conjugate(response_spec)), size, full_len)
    cross = complex_times(conjugate(product_spec), grad_spec)
    cross = (jnp.sum(cross[0], axis=0, keepdims=True), jnp.sum(cross[1], axis=0, keepdims=True))
    grad_response = inverse(cross, size, full_len)[0]
    grad_product = lax.all_to_all(
        grad_product_chan.astype(jnp.bfloat16), "seq", split_axis=1, concat_axis=2, tiled=True
    ).astype(jnp.float32)
    grad_short = jnp.concatenate([grad_query, grad_product * values, grad_product * keys], axis=-1)
    following = from_behind(grad_short[:, :2, :].astype(jnp.bfloat16), "seq", -1).astype(
        jnp.float32
    )
    grad_extended = jnp.concatenate([grad_short, following], axis=1)
    grad_mixed = (
        conv_taps[0] * grad_extended[:, :local_len]
        + conv_taps[1] * grad_extended[:, 1 : local_len + 1]
        + conv_taps[2] * grad_extended[:, 2:]
    )
    grad_taps = jnp.stack(
        [
            jnp.sum(grad_short * extended[:, 2:], axis=(0, 1)),
            jnp.sum(grad_short * extended[:, 1:-1], axis=(0, 1)),
            jnp.sum(grad_short * extended[:, :-2], axis=(0, 1)),
        ]
    )
    grad_mixed_low = grad_mixed.astype(jnp.bfloat16)
    term_in = jnp.einsum("btd,bte->de", normed, grad_mixed_low, preferred_element_type=jnp.float32)
    grad_normed = jnp.einsum(
        "bte,de->btd", grad_mixed_low, w_in, preferred_element_type=jnp.float32
    )
    mixer_terms = (
        lax.psum_scatter(
            term_in.astype(jnp.bfloat16), "seq", scatter_dimension=0, tiled=True
        ).astype(jnp.float32),
        lax.psum_scatter(
            term_out.astype(jnp.bfloat16), "seq", scatter_dimension=0, tiled=True
        ).astype(jnp.float32),
    )
    grad_hidden, grad_norm_gain = norm_back(hidden, scale_one, norm_gain, grad_normed)
    grad_tokens = (grad_hidden + grad_middle).astype(jnp.bfloat16)

    def response_of(residue_in, decay_in):
        return mode_response(residue_in, decay_in, full_len)

    unused, pull = jax.vjp(response_of, residue_part, decay_part)
    grad_residue_part, grad_decay_part = pull(grad_response)
    grad_residue = lax.dynamic_update_slice_in_dim(
        jnp.zeros_like(filter_residue), grad_residue_part, start, 0
    )
    grad_decay = lax.dynamic_update_slice_in_dim(
        jnp.zeros_like(filter_decay), grad_decay_part, start, 0
    )
    small = lax.psum(
        (grad_norm_gain, grad_taps, grad_residue, grad_decay, grad_feed_gain), ("dp", "seq")
    )
    large = (
        lax.psum(mixer_terms[0].astype(jnp.bfloat16), "dp").astype(jnp.float32),
        lax.psum(mixer_terms[1].astype(jnp.bfloat16), "dp").astype(jnp.float32),
        lax.psum(feed_terms[0].astype(jnp.bfloat16), "dp").astype(jnp.float32),
        lax.psum(feed_terms[1].astype(jnp.bfloat16), "dp").astype(jnp.float32),
        lax.psum(feed_terms[2].astype(jnp.bfloat16), "dp").astype(jnp.float32),
    )
    return (
        output,
        grad_tokens,
        small[0],
        large[0],
        small[1],
        small[2],
        small[3],
        large[1],
        small[4],
        large[2],
        large[3],
        large[4],
    )


def solution(mesh):
    placed = (
        P("dp", "seq", None),
        P("dp"),
        P(),
        P("seq", None),
        P(),
        P(),
        P(),
        P("seq", None),
        P(),
        P("seq", None),
        P("seq", None),
        P("seq", None),
        P("dp", "seq", None),
    )
    return jax.shard_map(
        body,
        mesh=mesh,
        in_specs=placed,
        out_specs=(
            P("dp", "seq", None),
            P("dp", "seq", None),
            P(),
            P("seq", None),
            P(),
            P(),
            P(),
            P("seq", None),
            P(),
            P("seq", None),
            P("seq", None),
            P("seq", None),
        ),
        check_vma=False,
    )
```

profile of v0, /device:TPU:0, one launch (start us, length us, event | category | flops | bytes accessed | tf_op | source)
XLA Modules:
  0.0 4133.8 jit_solution(7491863182339162644)
XLA Ops:
  19.6 473.1 %all-gather.6.cloned.1.call-done = bf16[2048,6144]{1,0:T(8,128)(2,1)} async-done(((bf16[256,6144]{1,0:T(8,128)(2,1)}), bf16[2048,6144]{1,0:T(8,128)(2,1)}) %all-gather.6.cloned.1.call-update) | async-done | bytes 25165840 | tf_op jit(solution)/shard_map/all_gather | solution.py:133
  492.7 11.9 fusion.20
  508.8 25.4 collective-permute-done
  553.0 6.2 fusion.115
  569.1 15.1 fusion.425
  598.3 7.0 fusion.60
  605.4 6.3 fusion.58
  611.7 6.9 fusion.82
  618.6 6.7 fusion.85
  640.2 8.6 fusion.36
  648.7 9.0 fusion.46
  657.7 6.5 subtract_bitcast_fusion.1
  668.9 11.7 all-to-all-start.1
  680.7 277.2 %all-gather.14.cloned.1.call-done = bf16[5632,2048]{1,0:T(8,128)(2,1)} async-done(((bf16[704,2048]{1,0:T(8,128)(2,1)}), bf16[5632,2048]{1,0:T(8,128)(2,1)}) %all-gather.14.cloned.1.call-update) | async-done | bytes 23068688 | tf_op jit(solution)/shard_map/all_gather | solution.py:137
  957.9 13.5 fusion.4
  976.2 109.8 %all-gather.8.cloned.1.call-done = bf16[2048,2048]{1,0:T(8,128)(2,1)} async-done(((bf16[256,2048]{1,0:T(8,128)(2,1)}), bf16[2048,2048]{1,0:T(8,128)(2,1)}) %all-gather.8.cloned.1.call-update) | async-done | bytes 8388624 | tf_op jit(solution)/shard_map/all_gather | solution.py:134
  1085.9 6.2 multiply_reduce_fusion.8
  1092.4 434.2 %all-gather.12.cloned.1.call-done = bf16[2048,5632]{1,0:T(8,128)(2,1)} async-done(((bf16[256,5632]{1,0:T(8,128)(2,1)}), bf16[2048,5632]{1,0:T(8,128)(2,1)}) %all-gather.12.cloned.1.call-update) | async-done | bytes 23068688 | tf_op jit(solution)/shard_map/all_gather | solution.py:136
  1526.7 13.3 fusion.10
  1539.9 429.2 %all-gather.10.cloned.1.call-done = bf16[2048,5632]{1,0:T(8,128)(2,1)} async-done(((bf16[256,5632]{1,0:T(8,128)(2,1)}), bf16[2048,5632]{1,0:T(8,128)(2,1)}) %all-gather.10.cloned.1.call-update) | async-done | bytes 23068688 | tf_op jit(solution)/shard_map/all_gather | solution.py:135
  1969.2 20.0 multiply_convert_fusion.1
  1989.2 12.8 fusion.8
  2001.9 13.7 multiply_reduce_fusion.6
  2024.9 13.1 bitcast_convert_fusion.3
  2038.0 13.2 bitcast_convert_fusion.2
  2052.4 13.2 bitcast_convert_fusion.1
  2065.7 8.6 fusion.423
  2075.0 50.2 %all_to_all.16 = bf16[2,128,2048]{1,0,2:T(2,128)(2,1)S(1)} all-to-all(bf16[2,128,2048]{1,0,2:T(2,128)(2,1)S(1)} %copy.189), channel_id=1, replica_groups=mesh['dp'=4,'seq'=8] {'seq'}, dimensions={2} | all-to-all | bytes 2097152 | tf_op jit(solution)/shard_map/all_to_all | solution.py:204
  2133.1 7.1 fusion.52
  2140.3 7.0 fusion.50
  2147.3 6.7 fusion.88
  2154.0 15.7 fusion.31
  2169.8 6.5 fusion.196
  2186.6 8.7 fusion.26
  2195.3 9.0 fusion.42
  2204.3 6.5 subtract_bitcast_fusion
  2214.5 57.3 %all_to_all.17 = bf16[2,1024,256]{2,0,1:T(2,128)(2,1)S(1)} all-to-all(bf16[2,1024,256]{2,0,1:T(2,128)(2,1)S(1)} %copy.201), channel_id=1, replica_groups=mesh['dp'=4,'seq'=8] {'seq'}, dimensions={1} | all-to-all | bytes 2097152 | tf_op jit(solution)/shard_map/all_to_all | solution.py:212
  2286.2 18.1 multiply_reduce_fusion.5
  2304.3 13.9 bitcast_convert_fusion
  2320.0 12.9 fusion.77
  2333.0 262.2 %reduce-scatter.10.cloned.1.call-done = bf16[256,5632]{1,0:T(8,128)(2,1)} async-done(((bf16[2048,5632]{1,0:T(8,128)(2,1)}), bf16[256,5632]{1,0:T(8,128)(2,1)}) %reduce-scatter.10.cloned.1.call-update) | async-done | bytes 2883600 | tf_op jit(solution)/shard_map/reduce_scatter | solution.py:187
  2595.1 377.1 %reduce-scatter.12.cloned.1.call-done = bf16[256,5632]{1,0:T(8,128)(2,1)} async-done(((bf16[2048,5632]{1,0:T(8,128)(2,1)}), bf16[256,5632]{1,0:T(8,128)(2,1)}) %reduce-scatter.12.cloned.1.call-update) | async-done | bytes 2883600 | tf_op jit(solution)/shard_map/reduce_scatter | solution.py:190
  2972.2 377.0 %reduce-scatter.14.cloned.1.call-done = bf16[704,2048]{1,0:T(8,128)(2,1)} async-done(((bf16[5632,2048]{1,0:T(8,128)(2,1)}), bf16[704,2048]{1,0:T(8,128)(2,1)}) %reduce-scatter.14.cloned.1.call-update) | async-done | bytes 2883600 | tf_op jit(solution)/shard_map/reduce_scatter | solution.py:193
  3349.2 407.1 %reduce-scatter.6.cloned.1.call-done = bf16[256,6144]{1,0:T(8,128)(2,1)} async-done(((bf16[2048,6144]{1,0:T(8,128)(2,1)}), bf16[256,6144]{1,0:T(8,128)(2,1)}) %reduce-scatter.6.cloned.1.call-update) | async-done | bytes 3145744 | tf_op jit(solution)/shard_map/reduce_scatter | solution.py:238
  3781.1 13.9 fusion.107
  3799.1 41.1 all-reduce.3
  3840.2 146.3 %all-reduce.11.cloned.1.call-done = (bf16[256,6144]{1,0:T(8,128)(2,1)}, bf16[256,2048]{1,0:T(8,128)(2,1)}, bf16[256,5632]{1,0:T(8,128)(2,1)}, bf16[256,5632]{1,0:T(8,128)(2,1)}, bf16[704,2048]{1,0:T(8,128)(2,1)}) async-done(((bf16[256,6144]{1,0:T(8,128)(2,1)}, bf16[256,2048]{1,0:T(8,128)(2,1)}, bf16[256,5632]{1,0:T(8,128)(2,1)}, bf16[256,5632]{1,0:T(8,128)(2,1)}, bf16[704,2048]{1,0:T(8,128)(2,1)}), ...) | async-done | bytes 12845072 | tf_op jit(solution)/shard_map/psum | solution.py:263
  4003.3 118.5 %all-reduce.9.cloned.1.call-done = (f32[3,6144]{1,0:T(4,128)}, f32[2048,16]{0,1:T(8,128)}, f32[2048,16]{0,1:T(8,128)}) async-done(((f32[3,6144]{1,0:T(4,128)}, f32[2048,16]{0,1:T(8,128)}, f32[2048,16]{0,1:T(8,128)}), (f32[3,6144]{1,0:T(4,128)}, f32[2048,16]{0,1:T(8,128)}, f32[2048,16]{0,1:T(8,128)})) %all-reduce.9.cloned.1.call-update) | async-done | bytes 335888 | tf_op jit(solution)/shard_map/psum | solution.py:259
  (241 shorter events, 182.9 us)
Async XLA Ops:
  7.2 485.5 %all-gather.6.cloned.1.call-start = ((), (), s32[]{:S(2)}) async-start(), calls=%async_computation.9 | async-start | bytes 28311552 | tf_op jit(solution)/shard_map/all_gather | solution.py:133
  7.9 950.0 %all-gather.14.cloned.1.call-start = ((), (), s32[]{:S(2)}) async-start(), calls=%async_computation.13 | async-start | bytes 25952256 | tf_op jit(solution)/shard_map/all_gather | solution.py:137
  8.7 1077.3 %all-gather.8.cloned.1.call-start = ((), (), s32[]{:S(2)}) async-start(), calls=%async_computation.10 | async-start | bytes 9437184 | tf_op jit(solution)/shard_map/all_gather | solution.py:134
  9.4 1517.3 %all-gather.12.cloned.1.call-start = ((), (), s32[]{:S(2)}) async-start(), calls=%async_computation.12 | async-start | bytes 25952256 | tf_op jit(solution)/shard_map/all_gather | solution.py:136
  10.0 1959.2 %all-gather.10.cloned.1.call-start = ((), (), s32[]{:S(2)}) async-start(), calls=%async_computation.11 | async-start | bytes 25952256 | tf_op jit(solution)/shard_map/all_gather | solution.py:135
  14.2 478.5 %copy-start.47 = (f32[2048]{0:T(1024)S(1)}, f32[2048]{0:T(1024)}, u32[]{:S(2)}) copy-start(f32[2048]{0:T(1024)} %param.15) | copy-start | bytes 24580
  14.6 625.5 %copy-start.30 = (f32[32,64]{0,1:T(8,128)}, f32[32,64]{0,1:T(8,128)S(1)}, u32[]{:S(2)}) copy-start(f32[32,64]{0,1:T(8,128)S(1)} %get-tuple-element.67) | copy-start | bytes 24580
  14.6 625.5 %copy-start.32 = (f32[32,64]{0,1:T(8,128)}, f32[32,64]{0,1:T(8,128)S(1)}, u32[]{:S(2)}) copy-start(f32[32,64]{0,1:T(8,128)S(1)} %get-tuple-element.68) | copy-start | bytes 24580
  14.9 489.7 %copy-start.50 = (f32[2,128]{1,0:T(2,128)}, f32[2,128]{1,0:T(2,128)S(1)}, u32[]{:S(2)}) copy-start(f32[2,128]{1,0:T(2,128)S(1)} %add_rsqrt_fusion.1) | copy-start | bytes 3076
  19.6 517.5 %copy-start.41 = (f32[1,6144]{1,0:T(1,128)}, f32[1,6144]{1,0:T(1,128)S(1)}, u32[]{:S(2)}) copy-start(f32[1,6144]{1,0:T(1,128)S(1)} %get-tuple-element.53) | copy-start | bytes 73732
  19.6 517.5 %copy-start.43 = (f32[1,6144]{1,0:T(1,128)}, f32[1,6144]{1,0:T(1,128)S(1)}, u32[]{:S(2)}) copy-start(f32[1,6144]{1,0:T(1,128)S(1)} %get-tuple-element.54) | copy-start | bytes 73732
  19.6 517.5 %copy-start.45 = (f32[1,6144]{1,0:T(1,128)}, f32[1,6144]{1,0:T(1,128)S(1)}, u32[]{:S(2)}) copy-start(f32[1,6144]{1,0:T(1,128)S(1)} %get-tuple-element.55) | copy-start | bytes 73732
  506.3 27.9 collective-permute-start
  508.8 85.5 %copy-start.37 = (f32[64,32]{0,1:T(8,128)}, f32[64,32]{0,1:T(8,128)S(1)}, u32[]{:S(2)}) copy-start(f32[64,32]{0,1:T(8,128)S(1)} %get-tuple-element.63) | copy-start | bytes 24580
  508.8 85.5 %copy-start.39 = (f32[64,32]{0,1:T(8,128)}, f32[64,32]{0,1:T(8,128)S(1)}, u32[]{:S(2)}) copy-start(f32[64,32]{0,1:T(8,128)S(1)} %get-tuple-element.64) | copy-start | bytes 24580
  547.4 38.1 all-to-all-start
  569.1 71.0 %copy-start = (f32[32,64,256]{2,0,1:T(8,128)}, f32[32,64,256]{2,0,1:T(8,128)S(1)}, u32[]{:S(2)}) copy-start(f32[32,64,256]{2,0,1:T(8,128)S(1)} %subtract_bitcast_fusion.3) | copy-start | bytes 6291460
  618.6 21.5 copy-start.3
  618.6 6.7 copy-start.8
  625.3 14.8 copy-start.5
  666.6 14.0 copy-start.60
  666.6 291.3 %copy-start.24 = (bf16[2,128,2048]{2,1,0:T(8,128)(2,1)S(1)}, bf16[2,128,2048]{2,1,0:T(8,128)(2,1)}, u32[]{:S(2)}) copy-start(bf16[2,128,2048]{2,1,0:T(8,128)(2,1)} %param.25) | copy-start | bytes 3145732
  668.9 302.5 %all-to-all-start.1 = ((bf16[2,1024,256]{2,0,1:T(2,128)(2,1)}), bf16[2,1024,256]{2,0,1:T(2,128)(2,1)S(1)}, u32[]{:S(2)}, u32[]{:S(2)}) async-start(bf16[2,1024,256]{2,0,1:T(2,128)(2,1)} %copy.186), calls=%async_computation.1 | async-start | bytes 2097152 | tf_op jit(solution)/shard_map/all_to_all | solution.py:162
  680.6 1652.4 %reduce-scatter.8.cloned.1.call-start = ((), (), s32[]{:S(2)}) async-start(), calls=%async_computation.15 | async-start | bytes 9437184 | tf_op jit(solution)/shard_map/reduce_scatter | solution.py:241
  976.2 116.0 %copy-start.52 = (f32[2048]{0:T(1024)S(1)}, f32[2048]{0:T(1024)}, u32[]{:S(2)}) copy-start(f32[2048]{0:T(1024)} %param.21) | copy-start | bytes 24580
  1092.1 909.8 %copy-start.21 = (f32[2,128,2048]{2,1,0:T(8,128)}, f32[2,128,2048]{2,1,0:T(8,128)S(1)}, u32[]{:S(2)}) copy-start(f32[2,128,2048]{2,1,0:T(8,128)S(1)} %get-tuple-element.57) | copy-start | bytes 6291460
  2019.1 46.6 %copy-start.11 = (f32[2,128,2048]{2,1,0:T(8,128)}, f32[2,128,2048]{2,1,0:T(8,128)S(1)}, u32[]{:S(2)}) copy-start(f32[2,128,2048]{2,1,0:T(8,128)S(1)} %subtract_add_fusion) | copy-start | bytes 6291460
  2024.8 570.3 %reduce-scatter.10.cloned.1.call-start = ((), (), s32[]{:S(2)}) async-start(), calls=%async_computation.16 | async-start | bytes 25952256 | tf_op jit(solution)/shard_map/reduce_scatter | solution.py:187
  2037.9 934.3 %reduce-scatter.12.cloned.1.call-start = ((), (), s32[]{:S(2)}) async-start(), calls=%async_computation.17 | async-start | bytes 25952256 | tf_op jit(solution)/shard_map/reduce_scatter | solution.py:190
  2051.2 1298.0 %reduce-scatter.14.cloned.1.call-start = ((), (), s32[]{:S(2)}) async-start(), calls=%async_computation.18 | async-start | bytes 25952256 | tf_op jit(solution)/shard_map/reduce_scatter | solution.py:193
  2065.6 1690.6 %reduce-scatter.6.cloned.1.call-start = ((), (), s32[]{:S(2)}) async-start(), calls=%async_computation.14 | async-start | bytes 28311552 | tf_op jit(solution)/shard_map/reduce_scatter | solution.py:238
  2133.1 14.2 copy-start.9
  2147.3 6.7 copy-start.4
  2147.3 6.7 copy-start.6
  2154.0 15.8 copy-start.1
  2169.8 6.5 copy-start.7
  2213.2 59.2 %slice-start = ((s8[6291456]{0:T(1024)(128)(4,1)}), s8[4194304]{0:T(1024)(128)(4,1)S(1)}, s32[]{:S(2)}) async-start(s8[6291456]{0:T(1024)(128)(4,1)} %bitcast.429), calls=%async_computation.21 | async-start | bytes 8388608
  2274.5 8.3 copy-start.14
  2274.5 8.3 copy-start.15
  2275.8 7.0 collective-permute-start.1
  2286.2 18.1 copy-start.20
  2286.2 18.1 copy-start.48
  2286.2 18.1 copy-start.51
  2318.2 1668.3 %all-reduce.11.cloned.1.call-start = ((), (), s32[]{:S(2)}) async-start(), calls=%async_computation.20 | async-start | bytes 25690112 | tf_op jit(solution)/shard_map/psum | solution.py:263
  3756.3 365.4 %all-reduce.9.cloned.1.call-start = ((), (), s32[]{:S(2)}) async-start(), calls=%async_computation.19 | async-start | bytes 720896 | tf_op jit(solution)/shard_map/psum | solution.py:259
  3781.0 14.0 copy-start.36
  3781.1 14.0 copy-start.35
  3781.1 14.7 copy-start.12
  (31 other events, 93.0 us)
Sparse Core Ops, SparseCore 0:
  9.5 483.1 all-gather.5
  494.2 463.6 all-gather.13
  960.0 125.8 all-gather.7
  1087.3 439.2 all-gather.11
  1528.0 441.0 all-gather.9
  2024.9 169.6 reduce-scatter.7
  2199.0 396.0 reduce-scatter.9
  2599.5 372.6 reduce-scatter.11
  2976.6 372.5 reduce-scatter.13
  3353.4 402.8 reduce-scatter.5
  3759.6 226.8 all-reduce.10
  3993.6 128.0 all-reduce.8
where the time goes:
time: 4140 us; the launch traced here: 4130 us
  waiting for transfers between devices  3450 us (83%)
  matrix products  394 us (10%)
  blocking collectives  149 us (4%)
  other arithmetic  66.7 us (2%)
    all_gather x1, waiting for transfers between devices, body(): lax.all_gather(in_weight, 'seq', axis=0, tiled=True)  473 us
    all_gather x1, waiting for transfers between devices, body(): lax.all_gather(up_weight, 'seq', axis=0, tiled=True)  434 us
    all_gather x1, waiting for transfers between devices, body(): lax.all_gather(gate_weight, 'seq', axis=0, tiled=True)  429 us
    reduce_scatter x1, waiting for transfers between devices, body(): lax.psum_scatter(term_in.astype(jnp.bfloat16), 'seq', scatter_dimension=0...  407 us
    reduce_scatter x1, waiting for transfers between devices, body(): lax.psum_scatter(term_up.astype(jnp.bfloat16), 'seq', scatter_dimension=0...  377 us
    reduce_scatter x1, waiting for transfers between devices, body(): lax.psum_scatter(term_down.astype(jnp.bfloat16), 'seq', scatter_dimension...  377 us
    all_gather x1, waiting for transfers between devices, body(): lax.all_gather(down_weight, 'seq', axis=0, tiled=True)  277 us
    reduce_scatter x1, waiting for transfers between devices, body(): lax.psum_scatter(term_gate.astype(jnp.bfloat16), 'seq', scatter_dimension...  262 us
  transfers between devices with their start and end apart: 16, of which 14 were waited for; matrix products, arithmetic and copies ran while one was open for 10% of the time, Pallas kernels for 0%

commit v1 on v0

--- a/solution.py
+++ b/solution.py
@@ -257,7 +257,7 @@
         jnp.zeros_like(filter_decay), grad_decay_part, start, 0
     )
     small = lax.psum(
-        (grad_norm_gain, grad_taps, grad_residue, grad_decay, grad_feed_gain), ("dp", "seq")
+        lax.psum((grad_norm_gain, grad_taps, grad_residue, grad_decay, grad_feed_gain), "seq"), "dp"
     )
     large = (
         lax.psum(mixer_terms[0].astype(jnp.bfloat16), "dp").astype(jnp.float32),

time: 4140 us -> 4120 us (level)
    psum x1, waiting for transfers between devices: 118 us -> 47.6 us  [body(): lax.psum((grad_norm_gain, grad_taps, grad_residue, grad_decay, grad_feed_...]
  transfers between devices with their start and end apart: 16 -> 17, of which waited for: 14 -> 15; matrix products, arithmetic and copies ran while one was open for 10% -> 10% of each run, Pallas kernels for 0% -> 0%
where the time goes in v1:
time: 4120 us; the launch traced here: 4110 us
  waiting for transfers between devices  3420 us (83%)
  matrix products  394 us (10%)
  blocking collectives  156 us (4%)
  other arithmetic  66.7 us (2%)
    all_gather x1, waiting for transfers between devices, body(): lax.all_gather(in_weight, 'seq', axis=0, tiled=True)  473 us
    all_gather x1, waiting for transfers between devices, body(): lax.all_gather(up_weight, 'seq', axis=0, tiled=True)  434 us
    all_gather x1, waiting for transfers between devices, body(): lax.all_gather(gate_weight, 'seq', axis=0, tiled=True)  429 us
    reduce_scatter x1, waiting for transfers between devices, body(): lax.psum_scatter(term_in.astype(jnp.bfloat16), 'seq', scatter_dimension=0...  407 us
    reduce_scatter x1, waiting for transfers between devices, body(): lax.psum_scatter(term_down.astype(jnp.bfloat16), 'seq', scatter_dimension...  377 us
    reduce_scatter x1, waiting for transfers between devices, body(): lax.psum_scatter(term_up.astype(jnp.bfloat16), 'seq', scatter_dimension=0...  377 us
    all_gather x1, waiting for transfers between devices, body(): lax.all_gather(down_weight, 'seq', axis=0, tiled=True)  277 us
    reduce_scatter x1, waiting for transfers between devices, body(): lax.psum_scatter(term_gate.astype(jnp.bfloat16), 'seq', scatter_dimension...  251 us
  transfers between devices with their start and end apart: 17, of which 15 were waited for; matrix products, arithmetic and copies ran while one was open for 10% of the time, Pallas kernels for 0%

profile of v1, /device:TPU:0, one launch (start us, length us, event | category | flops | bytes accessed | tf_op | source)
XLA Modules:
  0.0 4107.6 jit_solution(5634616393108580330)
XLA Ops:
  19.6 473.1 %all-gather.6.cloned.1.call-done = bf16[2048,6144]{1,0:T(8,128)(2,1)} async-done(((bf16[256,6144]{1,0:T(8,128)(2,1)}), bf16[2048,6144]{1,0:T(8,128)(2,1)}) %all-gather.6.cloned.1.call-update) | async-done | bytes 25165840 | tf_op jit(solution)/shard_map/all_gather | solution.py:133
  492.7 11.9 fusion.20
  508.8 25.4 collective-permute-done
  569.2 15.1 fusion.425
  598.5 7.0 fusion.60
  605.6 6.3 fusion.58
  611.9 6.9 fusion.82
  618.8 6.7 fusion.85
  640.4 8.6 fusion.36
  648.9 9.0 fusion.46
  657.9 6.5 subtract_bitcast_fusion.1
  669.1 11.6 all-to-all-start.1
  680.8 277.1 %all-gather.14.cloned.1.call-done = bf16[5632,2048]{1,0:T(8,128)(2,1)} async-done(((bf16[704,2048]{1,0:T(8,128)(2,1)}), bf16[5632,2048]{1,0:T(8,128)(2,1)}) %all-gather.14.cloned.1.call-update) | async-done | bytes 23068688 | tf_op jit(solution)/shard_map/all_gather | solution.py:137
  957.9 13.5 fusion.4
  976.2 109.8 %all-gather.8.cloned.1.call-done = bf16[2048,2048]{1,0:T(8,128)(2,1)} async-done(((bf16[256,2048]{1,0:T(8,128)(2,1)}), bf16[2048,2048]{1,0:T(8,128)(2,1)}) %all-gather.8.cloned.1.call-update) | async-done | bytes 8388624 | tf_op jit(solution)/shard_map/all_gather | solution.py:134
  1092.4 434.2 %all-gather.12.cloned.1.call-done = bf16[2048,5632]{1,0:T(8,128)(2,1)} async-done(((bf16[256,5632]{1,0:T(8,128)(2,1)}), bf16[2048,5632]{1,0:T(8,128)(2,1)}) %all-gather.12.cloned.1.call-update) | async-done | bytes 23068688 | tf_op jit(solution)/shard_map/all_gather | solution.py:136
  1526.7 13.3 fusion.10
  1539.9 429.2 %all-gather.10.cloned.1.call-done = bf16[2048,5632]{1,0:T(8,128)(2,1)} async-done(((bf16[256,5632]{1,0:T(8,128)(2,1)}), bf16[2048,5632]{1,0:T(8,128)(2,1)}) %all-gather.10.cloned.1.call-update) | async-done | bytes 23068688 | tf_op jit(solution)/shard_map/all_gather | solution.py:135
  1969.2 20.1 multiply_convert_fusion.1
  1989.2 12.8 fusion.8
  2002.0 13.8 multiply_reduce_fusion.6
  2025.0 13.1 bitcast_convert_fusion.3
  2038.2 13.2 bitcast_convert_fusion.2
  2052.6 13.1 bitcast_convert_fusion.1
  2065.8 8.6 fusion.423
  2075.2 50.3 %all_to_all.16 = bf16[2,128,2048]{1,0,2:T(2,128)(2,1)S(1)} all-to-all(bf16[2,128,2048]{1,0,2:T(2,128)(2,1)S(1)} %copy.189), channel_id=1, replica_groups=mesh['dp'=4,'seq'=8] {'seq'}, dimensions={2} | all-to-all | bytes 2097152 | tf_op jit(solution)/shard_map/all_to_all | solution.py:204
  2133.3 7.1 fusion.52
  2140.5 7.0 fusion.50
  2147.5 6.7 fusion.88
  2154.2 15.7 fusion.31
  2169.9 6.5 fusion.196
  2186.7 8.7 fusion.26
  2195.5 9.0 fusion.42
  2204.5 6.5 subtract_bitcast_fusion
  2214.7 57.4 %all_to_all.17 = bf16[2,1024,256]{2,0,1:T(2,128)(2,1)S(1)} all-to-all(bf16[2,1024,256]{2,0,1:T(2,128)(2,1)S(1)} %copy.201), channel_id=1, replica_groups=mesh['dp'=4,'seq'=8] {'seq'}, dimensions={1} | all-to-all | bytes 2097152 | tf_op jit(solution)/shard_map/all_to_all | solution.py:212
  2286.7 18.0 multiply_reduce_fusion.5
  2304.7 13.8 bitcast_convert_fusion
  2344.3 251.0 %reduce-scatter.10.cloned.1.call-done = bf16[256,5632]{1,0:T(8,128)(2,1)} async-done(((bf16[2048,5632]{1,0:T(8,128)(2,1)}), bf16[256,5632]{1,0:T(8,128)(2,1)}) %reduce-scatter.10.cloned.1.call-update) | async-done | bytes 2883600 | tf_op jit(solution)/shard_map/reduce_scatter | solution.py:187
  2595.4 376.5 %reduce-scatter.12.cloned.1.call-done = bf16[256,5632]{1,0:T(8,128)(2,1)} async-done(((bf16[2048,5632]{1,0:T(8,128)(2,1)}), bf16[256,5632]{1,0:T(8,128)(2,1)}) %reduce-scatter.12.cloned.1.call-update) | async-done | bytes 2883600 | tf_op jit(solution)/shard_map/reduce_scatter | solution.py:190
  2971.9 377.1 %reduce-scatter.14.cloned.1.call-done = bf16[704,2048]{1,0:T(8,128)(2,1)} async-done(((bf16[5632,2048]{1,0:T(8,128)(2,1)}), bf16[704,2048]{1,0:T(8,128)(2,1)}) %reduce-scatter.14.cloned.1.call-update) | async-done | bytes 2883600 | tf_op jit(solution)/shard_map/reduce_scatter | solution.py:193
  3349.0 407.2 %reduce-scatter.6.cloned.1.call-done = bf16[256,6144]{1,0:T(8,128)(2,1)} async-done(((bf16[2048,6144]{1,0:T(8,128)(2,1)}), bf16[256,6144]{1,0:T(8,128)(2,1)}) %reduce-scatter.6.cloned.1.call-update) | async-done | bytes 3145744 | tf_op jit(solution)/shard_map/reduce_scatter | solution.py:238
  3757.7 12.4 fusion.77
  3770.1 14.0 fusion.107
  3784.1 47.6 %all-reduce.12.cloned.1.call-done = (f32[3,6144]{1,0:T(4,128)}, f32[2048,16]{0,1:T(8,128)}, f32[2048,16]{0,1:T(8,128)}) async-done(((f32[3,6144]{1,0:T(4,128)}, f32[2048,16]{0,1:T(8,128)}, f32[2048,16]{0,1:T(8,128)}), (f32[3,6144]{1,0:T(4,128)}, f32[2048,16]{0,1:T(8,128)}, f32[2048,16]{0,1:T(8,128)})) %all-reduce.12.cloned.1.call-update) | async-done | bytes 335888 | tf_op jit(solution)/shard_map/psum | solution.py:260
  3835.1 35.4 all-reduce.3
  3870.5 12.5 all-reduce.5
  3883.0 177.5 %all-reduce.16.cloned.1.call-done = (bf16[256,6144]{1,0:T(8,128)(2,1)}, bf16[256,2048]{1,0:T(8,128)(2,1)}, bf16[256,5632]{1,0:T(8,128)(2,1)}, bf16[256,5632]{1,0:T(8,128)(2,1)}, bf16[704,2048]{1,0:T(8,128)(2,1)}) async-done(((bf16[256,6144]{1,0:T(8,128)(2,1)}, bf16[256,2048]{1,0:T(8,128)(2,1)}, bf16[256,5632]{1,0:T(8,128)(2,1)}, bf16[256,5632]{1,0:T(8,128)(2,1)}, bf16[704,2048]{1,0:T(8,128)(2,1)}), ...) | async-done | bytes 12845072 | tf_op jit(solution)/shard_map/psum | solution.py:263
  4077.3 18.6 all-reduce.14.cloned.1.call-done
  (245 shorter events, 195.7 us)
Async XLA Ops:
  7.2 485.5 %all-gather.6.cloned.1.call-start = ((), (), s32[]{:S(2)}) async-start(), calls=%async_computation.9 | async-start | bytes 28311552 | tf_op jit(solution)/shard_map/all_gather | solution.py:133
  7.9 950.0 %all-gather.14.cloned.1.call-start = ((), (), s32[]{:S(2)}) async-start(), calls=%async_computation.13 | async-start | bytes 25952256 | tf_op jit(solution)/shard_map/all_gather | solution.py:137
  8.7 1077.3 %all-gather.8.cloned.1.call-start = ((), (), s32[]{:S(2)}) async-start(), calls=%async_computation.10 | async-start | bytes 9437184 | tf_op jit(solution)/shard_map/all_gather | solution.py:134
  9.4 1517.3 %all-gather.12.cloned.1.call-start = ((), (), s32[]{:S(2)}) async-start(), calls=%async_computation.12 | async-start | bytes 25952256 | tf_op jit(solution)/shard_map/all_gather | solution.py:136
  10.0 1959.2 %all-gather.10.cloned.1.call-start = ((), (), s32[]{:S(2)}) async-start(), calls=%async_computation.11 | async-start | bytes 25952256 | tf_op jit(solution)/shard_map/all_gather | solution.py:135
  14.2 478.5 %copy-start.47 = (f32[2048]{0:T(1024)S(1)}, f32[2048]{0:T(1024)}, u32[]{:S(2)}) copy-start(f32[2048]{0:T(1024)} %param.15) | copy-start | bytes 24580
  14.6 625.8 %copy-start.30 = (f32[32,64]{0,1:T(8,128)}, f32[32,64]{0,1:T(8,128)S(1)}, u32[]{:S(2)}) copy-start(f32[32,64]{0,1:T(8,128)S(1)} %get-tuple-element.72) | copy-start | bytes 24580
  14.6 625.7 %copy-start.32 = (f32[32,64]{0,1:T(8,128)}, f32[32,64]{0,1:T(8,128)S(1)}, u32[]{:S(2)}) copy-start(f32[32,64]{0,1:T(8,128)S(1)} %get-tuple-element.73) | copy-start | bytes 24580
  14.9 489.7 %copy-start.50 = (f32[2,128]{1,0:T(2,128)}, f32[2,128]{1,0:T(2,128)S(1)}, u32[]{:S(2)}) copy-start(f32[2,128]{1,0:T(2,128)S(1)} %add_rsqrt_fusion.1) | copy-start | bytes 3076
  19.6 517.5 %copy-start.41 = (f32[1,6144]{1,0:T(1,128)}, f32[1,6144]{1,0:T(1,128)S(1)}, u32[]{:S(2)}) copy-start(f32[1,6144]{1,0:T(1,128)S(1)} %get-tuple-element.58) | copy-start | bytes 73732
  19.6 517.5 %copy-start.43 = (f32[1,6144]{1,0:T(1,128)}, f32[1,6144]{1,0:T(1,128)S(1)}, u32[]{:S(2)}) copy-start(f32[1,6144]{1,0:T(1,128)S(1)} %get-tuple-element.59) | copy-start | bytes 73732
  19.6 517.5 %copy-start.45 = (f32[1,6144]{1,0:T(1,128)}, f32[1,6144]{1,0:T(1,128)S(1)}, u32[]{:S(2)}) copy-start(f32[1,6144]{1,0:T(1,128)S(1)} %get-tuple-element.60) | copy-start | bytes 73732
  506.3 27.9 collective-permute-start
  508.8 85.7 %copy-start.37 = (f32[64,32]{0,1:T(8,128)}, f32[64,32]{0,1:T(8,128)S(1)}, u32[]{:S(2)}) copy-start(f32[64,32]{0,1:T(8,128)S(1)} %get-tuple-element.68) | copy-start | bytes 24580
  508.8 85.7 %copy-start.39 = (f32[64,32]{0,1:T(8,128)}, f32[64,32]{0,1:T(8,128)S(1)}, u32[]{:S(2)}) copy-start(f32[64,32]{0,1:T(8,128)S(1)} %get-tuple-element.69) | copy-start | bytes 24580
  547.5 38.2 all-to-all-start
  569.2 71.2 %copy-start = (f32[32,64,256]{2,0,1:T(8,128)}, f32[32,64,256]{2,0,1:T(8,128)S(1)}, u32[]{:S(2)}) copy-start(f32[32,64,256]{2,0,1:T(8,128)S(1)} %subtract_bitcast_fusion.3) | copy-start | bytes 6291460
  618.8 21.5 copy-start.3
  618.8 6.7 copy-start.8
  625.5 14.8 copy-start.5
  666.8 13.9 copy-start.60
  666.8 291.1 %copy-start.24 = (bf16[2,128,2048]{2,1,0:T(8,128)(2,1)S(1)}, bf16[2,128,2048]{2,1,0:T(8,128)(2,1)}, u32[]{:S(2)}) copy-start(bf16[2,128,2048]{2,1,0:T(8,128)(2,1)} %param.25) | copy-start | bytes 3145732
  669.1 302.3 %all-to-all-start.1 = ((bf16[2,1024,256]{2,0,1:T(2,128)(2,1)}), bf16[2,1024,256]{2,0,1:T(2,128)(2,1)S(1)}, u32[]{:S(2)}, u32[]{:S(2)}) async-start(bf16[2,1024,256]{2,0,1:T(2,128)(2,1)} %copy.186), calls=%async_computation.1 | async-start | bytes 2097152 | tf_op jit(solution)/shard_map/all_to_all | solution.py:162
  680.6 1663.7 %reduce-scatter.8.cloned.1.call-start = ((), (), s32[]{:S(2)}) async-start(), calls=%async_computation.15 | async-start | bytes 9437184 | tf_op jit(solution)/shard_map/reduce_scatter | solution.py:241
  976.2 116.0 %copy-start.52 = (f32[2048]{0:T(1024)S(1)}, f32[2048]{0:T(1024)}, u32[]{:S(2)}) copy-start(f32[2048]{0:T(1024)} %param.21) | copy-start | bytes 24580
  1092.1 909.9 %copy-start.21 = (f32[2,128,2048]{2,1,0:T(8,128)}, f32[2,128,2048]{2,1,0:T(8,128)S(1)}, u32[]{:S(2)}) copy-start(f32[2,128,2048]{2,1,0:T(8,128)S(1)} %get-tuple-element.62) | copy-start | bytes 6291460
  2019.2 46.6 %copy-start.11 = (f32[2,128,2048]{2,1,0:T(8,128)}, f32[2,128,2048]{2,1,0:T(8,128)S(1)}, u32[]{:S(2)}) copy-start(f32[2,128,2048]{2,1,0:T(8,128)S(1)} %subtract_add_fusion) | copy-start | bytes 6291460
  2025.0 570.4 %reduce-scatter.10.cloned.1.call-start = ((), (), s32[]{:S(2)}) async-start(), calls=%async_computation.16 | async-start | bytes 25952256 | tf_op jit(solution)/shard_map/reduce_scatter | solution.py:187
  2038.1 933.8 %reduce-scatter.12.cloned.1.call-start = ((), (), s32[]{:S(2)}) async-start(), calls=%async_computation.17 | async-start | bytes 25952256 | tf_op jit(solution)/shard_map/reduce_scatter | solution.py:190
  2051.4 1297.5 %reduce-scatter.14.cloned.1.call-start = ((), (), s32[]{:S(2)}) async-start(), calls=%async_computation.18 | async-start | bytes 25952256 | tf_op jit(solution)/shard_map/reduce_scatter | solution.py:193
  2065.8 1690.4 %reduce-scatter.6.cloned.1.call-start = ((), (), s32[]{:S(2)}) async-start(), calls=%async_computation.14 | async-start | bytes 28311552 | tf_op jit(solution)/shard_map/reduce_scatter | solution.py:238
  2133.3 14.2 copy-start.9
  2147.5 6.7 copy-start.4
  2147.5 6.7 copy-start.6
  2154.2 15.7 copy-start.1
  2169.9 6.5 copy-start.7
  2213.4 59.3 %slice-start = ((s8[6291456]{0:T(1024)(128)(4,1)}), s8[4194304]{0:T(1024)(128)(4,1)S(1)}, s32[]{:S(2)}) async-start(s8[6291456]{0:T(1024)(128)(4,1)} %bitcast.429), calls=%async_computation.22 | async-start | bytes 8388608
  2274.7 8.5 copy-start.14
  2274.7 8.5 copy-start.15
  2276.0 7.2 collective-permute-start.1
  2286.7 18.0 copy-start.20
  2286.7 18.0 copy-start.48
  2286.7 18.0 copy-start.51
  2318.5 1513.2 %all-reduce.12.cloned.1.call-start = ((), (), s32[]{:S(2)}) async-start(), calls=%async_computation.19 | async-start | bytes 720896 | tf_op jit(solution)/shard_map/psum | solution.py:260
  2344.3 1716.3 %all-reduce.16.cloned.1.call-start = ((), (), s32[]{:S(2)}) async-start(), calls=%async_computation.21 | async-start | bytes 25690112 | tf_op jit(solution)/shard_map/psum | solution.py:263
  3756.2 339.8 %all-reduce.14.cloned.1.call-start = ((), (), s32[]{:S(2)}) async-start(), calls=%async_computation.20 | async-start | bytes 720896 | tf_op jit(solution)/shard_map/psum | solution.py:259
  3770.1 61.6 %copy-start.12 = (f32[2,128,2048]{2,1,0:T(8,128)S(1)}, f32[2,128,2048]{2,1,0:T(8,128)}, u32[]{:S(2)}) copy-start(f32[2,128,2048]{2,1,0:T(8,128)} %copy-done.11) | copy-start | bytes 6291460
  3784.1 51.0 %copy-start.57 = (f32[2048]{0:T(1024)S(1)}, f32[2048]{0:T(1024)}, u32[]{:S(2)}) copy-start(f32[2048]{0:T(1024)} %get-tuple-element.17) | copy-start | bytes 24580
  (32 other events, 91.2 us)
Sparse Core Ops, SparseCore 0:
  9.5 483.1 all-gather.5
  494.2 463.6 all-gather.13
  960.0 125.8 all-gather.7
  1087.3 439.2 all-gather.11
  1528.0 441.0 all-gather.9
  2025.1 169.6 reduce-scatter.7
  2199.2 396.1 reduce-scatter.9
  2599.7 372.1 reduce-scatter.11
  2976.3 372.6 reduce-scatter.13
  3353.2 402.9 reduce-scatter.5
  3760.8 70.8 all-reduce.11
  3834.6 225.8 all-reduce.15
  4063.1 32.8 all-reduce.13
